TPU v7x, 32 devices: a whole 2x2x4 slice. The times are simulated.
32 devices in a mesh: dp: 8 (over y, x, core), seq: 4 (over z).
Axes of the slice: x: 2, y: 2, z: 4, core: 2. Of those that a mesh axis runs over, the one named last changes fastest.
Arguments:
- hidden: bfloat16 [8192, 1792], P(('dp', 'seq')), may hold values from -12.75 to 12.75
- depths: int32 [8192], P(('dp', 'seq')), may hold values from 1 to 3, as said below
- packed_slot_index: int32 [8192], P(('dp', 'seq')), may hold values from -1 to 511, as said below
- value_weight: bfloat16 [1792, 1024], P('dp'), may hold values from -0.125 to 0.125
- output_weight: bfloat16 [1024, 1792], P('dp'), may hold values from -0.1875 to 0.1875
- adapter_down_factor: bfloat16 [1792, 128], P('dp'), may hold values from -0.125 to 0.125
- adapter_up_factor: bfloat16 [1024, 128], P('dp'), may hold values from -0.5 to 0.5
- before_norm_gain: float32 [1792], replicated, may hold values from 0.1 to 1.9
- after_norm_gain: float32 [1792], replicated, may hold values from 0.1 to 1.9
- cotangent: bfloat16 [4096, 1792], P(('dp', 'seq')), may hold values from -6 to 6
Outputs:
- looped: bfloat16 [4096, 1792], P(('dp', 'seq'))
- grad_hidden: bfloat16 [8192, 1792], P(('dp', 'seq'))
- down_factor_gradient: float32 [1792, 128], P('dp', 'seq')
- up_factor_gradient: float32 [1024, 128], P('dp', 'seq')
Inputs may be any that keep to these rules, and one draw needn't show every extreme that they name: `depths`: of the 1024 tokens of one dp index exactly 512 have depth 2 or 3, and all 256 tokens of one seq index are among them. -1 exactly where depths is 1. Over the tokens of one dp index with depth 2 or 3 the slots are a permutation of 0 to 511; packed_slot_index // 128 is the seq index that holds the token's packed row. At most 64 tokens of one device have slots of one seq index, and exactly 64 do in every dp index.
All inputs are finite; a program needn't handle non-finite values.
Results may differ from a plain program's by a relative error of at most 0.01.
Values may be sent and summed in bfloat16 or wider, within the bound.
A program may use at most 64 MiB of HBM per device.

v0:
```python
import math
import jax
import jax.numpy as jnp
from jax import lax
from jax.sharding import PartitionSpec as P

epsilon = 1e-06


def contract_final_axis(left, right):
    return lax.dot_general(
        left, right, (((1,), (1,)), ((), ())), preferred_element_type=jnp.float32
    )


def contract_first(left, right):
    return lax.dot_general(
        left, right, (((0,), (0,)), ((), ())), preferred_element_type=jnp.float32
    )


def layer_forward(
    input_rows,
    cotangent_rows,
    value_weight,
    output_weight,
    adapter_down_factor,
    adapter_up_factor,
    before_norm_gain,
    after_norm_gain,
):
    x_float = input_rows.astype(jnp.float32)
    inv_pre = lax.rsqrt(jnp.mean(x_float * x_float, axis=-1, keepdims=True) + epsilon)
    whitened = x_float * inv_pre
    normalized_rows = (whitened * before_norm_gain).astype(jnp.bfloat16)
    rank_reduced = jnp.dot(
        normalized_rows, adapter_down_factor, preferred_element_type=jnp.float32
    ).astype(jnp.bfloat16)
    projected_rows = (
        jnp.dot(normalized_rows, value_weight, preferred_element_type=jnp.float32)
        + contract_final_axis(rank_reduced, adapter_up_factor)
    ).astype(jnp.bfloat16)
    mixed_out = jnp.dot(projected_rows, output_weight, preferred_element_type=jnp.float32)
    inv_post = lax.rsqrt(jnp.mean(mixed_out * mixed_out, axis=-1, keepdims=True) + epsilon)
    shaped = mixed_out * inv_post
    looped = (x_float + shaped * after_norm_gain).astype(jnp.bfloat16)
    cot_float = cotangent_rows.astype(jnp.float32)
    grad_shaped = cot_float * after_norm_gain
    grad_mixed = (
        inv_post * (grad_shaped - shaped * jnp.mean(grad_shaped * shaped, axis=-1, keepdims=True))
    ).astype(jnp.bfloat16)
    value_gradient = contract_final_axis(grad_mixed, output_weight).astype(jnp.bfloat16)
    low_rank_gradient = jnp.dot(
        value_gradient, adapter_up_factor, preferred_element_type=jnp.float32
    ).astype(jnp.bfloat16)
    normalized_gradient = contract_final_axis(value_gradient, value_weight) + contract_final_axis(
        low_rank_gradient, adapter_down_factor
    )
    grad_white = normalized_gradient * before_norm_gain
    gradient_rows = (
        cot_float
        + inv_pre
        * (grad_white - whitened * jnp.mean(grad_white * whitened, axis=-1, keepdims=True))
    ).astype(jnp.bfloat16)
    down_factor_gradient = contract_first(normalized_rows, low_rank_gradient)
    up_factor_gradient = contract_first(value_gradient, rank_reduced)
    return (looped, gradient_rows, down_factor_gradient, up_factor_gradient)


def body(
    hidden,
    depths,
    packed_slot_index,
    value_weight,
    output_weight,
    adapter_down_factor,
    adapter_up_factor,
    before_norm_gain,
    after_norm_gain,
    cotangent,
):
    seq_count = lax.axis_size("seq")
    own_index = lax.axis_index("seq")
    tok_count = hidden.shape[0]
    act_rows = cotangent.shape[0]
    value_full, out_full, down_full, up_full = (
        lax.all_gather(value_weight, "dp", axis=0, tiled=True),
        lax.all_gather(output_weight, "dp", axis=0, tiled=True),
        lax.all_gather(adapter_down_factor, "dp", axis=0, tiled=True),
        lax.all_gather(adapter_up_factor, "dp", axis=0, tiled=True),
    )
    depth_all, slot_all = (
        lax.all_gather(depths, "seq", axis=0, tiled=True),
        lax.all_gather(packed_slot_index, "seq", axis=0, tiled=True),
    )
    active_all = depth_all >= 2
    dest_all = jnp.where(active_all, slot_all // act_rows, -1)
    pos_all = jnp.where(active_all, slot_all % act_rows, 0)
    mine = active_all & (dest_all == own_index)
    active = depths >= 2
    zero_row = jnp.zeros((), jnp.bfloat16)
    rows_all = lax.all_gather(hidden, "seq", axis=0, tiled=True)
    source = (
        jnp.zeros((act_rows,), jnp.int32)
        .at[jnp.where(mine, pos_all, act_rows)]
        .set(jnp.arange(seq_count * tok_count, dtype=jnp.int32), mode="drop")
    )
    packed = jnp.take(rows_all, source, axis=0)
    looped, gradient_rows, down_factor_gradient, up_factor_gradient = layer_forward(
        packed,
        cotangent,
        value_full,
        out_full,
        down_full,
        up_full,
        before_norm_gain,
        after_norm_gain,
    )
    grads_all = lax.all_gather(gradient_rows, "seq", axis=0, tiled=True)
    picked = jnp.take(grads_all, jnp.maximum(packed_slot_index, 0), axis=0)
    grad_hidden = jnp.where(active[:, None], picked, zero_row)
    grad_scale = 1.0 / math.sqrt(seq_count * act_rows * lax.axis_size("dp"))
    down_term = down_factor_gradient * grad_scale
    up_term = up_factor_gradient * grad_scale
    down_mid, up_mid = (
        lax.psum_scatter(
            down_term.astype(jnp.bfloat16), "seq", scatter_dimension=1, tiled=True
        ).astype(jnp.float32),
        lax.psum_scatter(
            up_term.astype(jnp.bfloat16), "seq", scatter_dimension=1, tiled=True
        ).astype(jnp.float32),
    )
    down_sum, up_sum = (
        lax.psum_scatter(down_mid, "dp", scatter_dimension=0, tiled=True),
        lax.psum_scatter(up_mid, "dp", scatter_dimension=0, tiled=True),
    )
    return (looped, grad_hidden, down_sum, up_sum)


def solution(mesh):
    placed = (
        P(("dp", "seq"), None),
        P(("dp", "seq")),
        P(("dp", "seq")),
        P("dp", None),
        P("dp", None),
        P("dp", None),
        P("dp", None),
        P(),
        P(),
        P(("dp", "seq"), None),
    )
    return jax.shard_map(
        body,
        mesh=mesh,
        in_specs=placed,
        out_specs=(P(("dp", "seq"), None), P(("dp", "seq"), None), P("dp", "seq"), P("dp", "seq")),
        check_vma=False,
    )
```

profile of v0, /device:TPU:0, one launch (start us, length us, event | category | flops | bytes accessed | tf_op | source)
XLA Modules:
  0.0 329.3 jit_solution(13722843027043391828)
XLA Ops:
  9.4 12.8 %all-gather = s32[4,1,256]{2,1,0:T(1,128)S(1)} all-gather(s32[1,1,256]{2,1,0:T(1,128)} %bitcast.21), channel_id=1, replica_groups=mesh['dp'=8,'seq'=4] {'seq'}, dimensions={0}, use_global_device_ids=true | all-gather | bytes 5120 | tf_op jit(solution)/shard_map/all_gather | solution.py:93
  22.3 8.1 %all-gather.1 = s32[4,1,256]{2,1,0:T(1,128)S(1)} all-gather(s32[1,1,256]{2,1,0:T(1,128)} %bitcast.20), channel_id=1, replica_groups=mesh['dp'=8,'seq'=4] {'seq'}, dimensions={0}, use_global_device_ids=true | all-gather | bytes 5120 | tf_op jit(solution)/shard_map/all_gather | solution.py:94
  30.4 4.3 %scatter_custom_fusion = s32[128]{0:T(128)S(1)} fusion(s32[1024]{0:T(1024)S(1)} %compare_select_fusion, s32[1024]{0:T(1024)S(1)} %iota.3, s32[]{:T(128)} %constant.69.clone.1), kind=kCustom, calls=%fused_computation.69 | custom fusion | bytes 516 | tf_op jit(solution)/shard_map/scatter | solution.py:106
  34.8 9.5 %all_gather.29 = bf16[1024,128]{1,0:T(8,128)(2,1)S(1)} all-gather(bf16[128,128]{1,0:T(8,128)(2,1)} %param.16), channel_id=1, replica_groups=mesh['dp'=8,'seq'=4] {'dp'}, dimensions={0}, use_global_device_ids=true | all-gather | bytes 294912 | tf_op jit(solution)/shard_map/all_gather | solution.py:90
  44.3 9.5 %all_gather.28 = bf16[1792,128]{1,0:T(8,128)(2,1)S(1)} all-gather(bf16[224,128]{1,0:T(8,128)(2,1)} %param.15), channel_id=1, replica_groups=mesh['dp'=8,'seq'=4] {'dp'}, dimensions={0}, use_global_device_ids=true | all-gather | bytes 516096 | tf_op jit(solution)/shard_map/all_gather | solution.py:89
  53.8 30.7 %all-gather.7.cloned.1.call-done = bf16[1024,1792]{1,0:T(8,128)(2,1)} async-done(((bf16[256,1792]{1,0:T(8,128)(2,1)}), bf16[1024,1792]{1,0:T(8,128)(2,1)}) %all-gather.7.cloned.1.call-update) | async-done | bytes 3670032 | tf_op jit(solution)/shard_map/all_gather | solution.py:102
  84.5 3.8 %gather_fusion = bf16[128,1792]{1,0:T(8,128)(2,1)S(1)} fusion(bf16[1024,1792]{1,0:T(8,128)(2,1)} %all-gather.7.cloned.1.call-done, s32[1024]{0:T(1024)S(1)} %pad_clamp_fusion.1), kind=kCustom, calls=%fused_computation | custom fusion | bytes 918016 | tf_op jit(solution)/shard_map/jit(_take)/gather | solution.py:108
  89.0 30.5 %all-gather.9.cloned.1.call-done = bf16[1792,1024]{1,0:T(8,128)(2,1)} async-done(((bf16[224,1024]{1,0:T(8,128)(2,1)}), bf16[1792,1024]{1,0:T(8,128)(2,1)}) %all-gather.9.cloned.1.call-update) | async-done | bytes 3670032 | tf_op jit(solution)/shard_map/all_gather | solution.py:87
  119.5 2.7 fusion.37
  122.3 33.7 %all-gather.11.cloned.1.call-done = bf16[1024,1792]{1,0:T(8,128)(2,1)} async-done(((bf16[128,1792]{1,0:T(8,128)(2,1)}), bf16[1024,1792]{1,0:T(8,128)(2,1)}) %all-gather.11.cloned.1.call-update) | async-done | bytes 3670032 | tf_op jit(solution)/shard_map/all_gather | solution.py:88
  156.0 2.9 multiply_reduce_fusion
  160.0 3.4 %convolution_convert_fusion = bf16[128,1024]{1,0:T(8,128)(2,1)S(1)} fusion(bf16[1024,1792]{1,0:T(8,128)(2,1)} %all-gather.11.cloned.1.call-done, bf16[128,1792]{1,0:T(8,128)(2,1)S(1)} %copy-done, f32[128,1792]{1,0:T(8,128)S(1)} %get-tuple-element.7, f32[128]{0:T(128)S(1)} %broadcast_multiply_fusion.1, f32[1792]{0:T(1024)S(1)} %copy-done.1, ...), kind=kOutput, calls=%fused_computation.15 | convolution fusion | flops 471498752 | bytes 5316608 | tf_op jit(solution)/shard_map/dot_general | solution.py:11
  163.6 1.2 fusion.1
  165.9 3.4 %fusion.39 = f32[128,1792]{1,0:T(8,128)S(1)} fusion(bf16[128,1024]{1,0:T(8,128)(2,1)S(1)} %convolution_convert_fusion, bf16[1792,1024]{1,0:T(8,128)(2,1)} %all-gather.9.cloned.1.call-done), kind=kOutput, calls=%fused_computation.72 | convolution fusion | flops 469762048 | bytes 4849664 | tf_op jit(solution)/shard_map/dot_general | solution.py:11
  169.8 16.2 %reduce-scatter.7.cloned.1.call-done = bf16[1792,32]{0,1:T(8,128)(2,1)} async-done(((bf16[1792,128]{0,1:T(8,128)(2,1)}), bf16[1792,32]{0,1:T(8,128)(2,1)}) %reduce-scatter.7.cloned.1.call-update) | async-done | bytes 114704 | tf_op jit(solution)/shard_map/reduce_scatter | solution.py:126
  186.0 2.0 copy.14
  188.1 1.3 fusion.13
  189.6 16.7 %reduce-scatter.9.cloned.1.call-done = bf16[1024,32]{0,1:T(8,128)(2,1)} async-done(((bf16[1024,128]{0,1:T(8,128)(2,1)}), bf16[1024,32]{0,1:T(8,128)(2,1)}) %reduce-scatter.9.cloned.1.call-update) | async-done | bytes 65552 | tf_op jit(solution)/shard_map/reduce_scatter | solution.py:129
  206.3 1.5 convert_element_type.55
  207.8 35.8 %reduce-scatter.13.cloned.1.call-done = f32[224,32]{1,0:T(8,128)} async-done(((f32[1792,32]{1,0:T(8,128)}), f32[224,32]{1,0:T(8,128)}) %reduce-scatter.13.cloned.1.call-update) | async-done | bytes 28688
  243.6 1.6 copy.15
  245.2 41.4 %all-gather.13.cloned.1.call-done = bf16[512,1792]{1,0:T(8,128)(2,1)} async-done(((bf16[128,1792]{1,0:T(8,128)(2,1)}), bf16[512,1792]{1,0:T(8,128)(2,1)}) %all-gather.13.cloned.1.call-update) | async-done | bytes 1835024 | tf_op jit(solution)/shard_map/all_gather | solution.py:119
  286.6 3.9 %gather_fusion.1 = bf16[256,1792]{1,0:T(8,128)(2,1)S(1)} fusion(bf16[512,1792]{1,0:T(8,128)(2,1)} %all-gather.13.cloned.1.call-done, s32[1024]{0:T(1024)S(1)} %pad_clamp_fusion), kind=kCustom, calls=%fused_computation.1 | custom fusion | bytes 1836032 | tf_op jit(solution)/shard_map/jit(_take)/gather | solution.py:120
  291.6 30.8 %reduce-scatter.11.cloned.1.call-done = f32[128,32]{0,1:T(8,128)} async-done(((f32[1024,32]{0,1:T(8,128)}), f32[128,32]{0,1:T(8,128)}) %reduce-scatter.11.cloned.1.call-update) | async-done | bytes 16400 | tf_op jit(solution)/shard_map/reduce_scatter | solution.py:135
  (48 shorter events, 7.1 us)
Async XLA Ops:
  7.2 81.5 %copy-start.2 = (f32[1792]{0:T(1024)S(1)}, f32[1792]{0:T(1024)}, u32[]{:S(2)}) copy-start(f32[1792]{0:T(1024)} %param.17) | copy-start | bytes 21508
  7.2 77.3 %all-gather.7.cloned.1.call-start = ((), (), s32[]{:S(2)}) async-start(), calls=%async_computation.4 | async-start | bytes 4587520 | tf_op jit(solution)/shard_map/all_gather | solution.py:102
  7.9 111.6 %all-gather.9.cloned.1.call-start = ((), (), s32[]{:S(2)}) async-start(), calls=%async_computation.5 | async-start | bytes 4128768 | tf_op jit(solution)/shard_map/all_gather | solution.py:87
  8.7 147.3 %all-gather.11.cloned.1.call-start = ((), (), s32[]{:S(2)}) async-start(), calls=%async_computation.6 | async-start | bytes 4128768 | tf_op jit(solution)/shard_map/all_gather | solution.py:88
  9.4 176.6 %reduce-scatter.7.cloned.1.call-start = ((), (), s32[]{:S(2)}) async-start(), calls=%async_computation.8 | async-start | bytes 573440 | tf_op jit(solution)/shard_map/reduce_scatter | solution.py:126
  122.3 36.7 %copy-start = (bf16[128,1792]{1,0:T(8,128)(2,1)S(1)}, bf16[128,1792]{1,0:T(8,128)(2,1)}, u32[]{:S(2)}) copy-start(bf16[128,1792]{1,0:T(8,128)(2,1)} %param.19) | copy-start | bytes 1376260
  122.3 36.6 %copy-start.1 = (f32[1792]{0:T(1024)S(1)}, f32[1792]{0:T(1024)}, u32[]{:S(2)}) copy-start(f32[1792]{0:T(1024)} %param.18) | copy-start | bytes 21508
  164.8 41.5 %reduce-scatter.9.cloned.1.call-start = ((), (), s32[]{:S(2)}) async-start(), calls=%async_computation.9 | async-start | bytes 327680 | tf_op jit(solution)/shard_map/reduce_scatter | solution.py:129
  165.8 77.8 %reduce-scatter.13.cloned.1.call-start = ((), (), s32[]{:S(2)}) async-start(), calls=%async_computation.11 | async-start | bytes 1032192
  169.3 20.2 %copy-start.3 = (s32[256]{0:T(256)S(1)}, s32[256]{0:T(256)}, u32[]{:S(2)}) copy-start(s32[256]{0:T(256)} %param.12) | copy-start | bytes 3076
  169.3 20.3 %copy-start.4 = (s32[256]{0:T(256)S(1)}, s32[256]{0:T(256)}, u32[]{:S(2)}) copy-start(s32[256]{0:T(256)} %param.11) | copy-start | bytes 3076
  188.0 98.6 %all-gather.13.cloned.1.call-start = ((), (), s32[]{:S(2)}) async-start(), calls=%async_computation.7 | async-start | bytes 2293760 | tf_op jit(solution)/shard_map/all_gather | solution.py:119
  189.4 133.0 %reduce-scatter.11.cloned.1.call-start = ((), (), s32[]{:S(2)}) async-start(), calls=%async_computation.10 | async-start | bytes 147456 | tf_op jit(solution)/shard_map/reduce_scatter | solution.py:135
Sparse Core Ops, SparseCore 0:
  9.6 74.8 all-gather.6
  86.4 33.0 all-gather.8
  121.4 34.5 all-gather.10
  164.9 20.9 reduce-scatter.6
  188.2 18.0 reduce-scatter.8
  209.9 33.6 reduce-scatter.12
  245.2 41.3 all-gather.12
  290.2 32.2 reduce-scatter.10
where the time goes:
time: 330 us; the launch traced here: 329 us
  waiting for transfers between devices  238 us (72%)
  blocking collectives  39.9 us (12%)
  local copies, waits for them, and re-layouts  15.7 us (5%)
  matrix products  15.5 us (5%)
  between operations  14.3 us (4%)
  other arithmetic  5.43 us (2%)
    all_gather x1, waiting for transfers between devices, body(): grads_all = lax.all_gather(gradient_rows, 'seq', axis=0, tiled=True)  41.4 us
    unnamed x9, waiting for transfers between devices  38 us
    all_gather x1, waiting for transfers between devices, body(): lax.all_gather(output_weight, 'dp', axis=0, tiled=True)  33.7 us
    reduce_scatter x1, waiting for transfers between devices, body(): lax.psum_scatter(up_mid, 'dp', scatter_dimension=0, tiled=True)  30.8 us
    all_gather x1, waiting for transfers between devices, body(): rows_all = lax.all_gather(hidden, 'seq', axis=0, tiled=True)  30.7 us
    all_gather x1, waiting for transfers between devices, body(): lax.all_gather(value_weight, 'dp', axis=0, tiled=True)  30.5 us
    reduce_scatter x1, waiting for transfers between devices, body(): lax.psum_scatter(up_term.astype(jnp.bfloat16), 'seq', scatter_dimension=1...  16.7 us
    reduce_scatter x1, waiting for transfers between devices, body(): lax.psum_scatter(down_term.astype(jnp.bfloat16), 'seq', scatter_dimension...  16.2 us
  transfers between devices with their start and end apart: 8, of which 8 were waited for; matrix products, arithmetic and copies ran while one was open for 8% of the time, Pallas kernels for 0%

commit v1 on v0

--- a/solution.py
+++ b/solution.py
@@ -116,7 +116,12 @@
         before_norm_gain,
         after_norm_gain,
     )
-    grads_all = lax.all_gather(gradient_rows, "seq", axis=0, tiled=True)
+    ring = [gradient_rows]
+    for hop in range(3):
+        ring.append(lax.ppermute(ring[-1], "seq", [(dev, (dev + 1) % 4) for dev in range(4)]))
+    grads_all = jnp.roll(
+        jnp.concatenate(ring[::-1], axis=0), (lax.axis_index("seq") + 1) * ring[0].shape[0], axis=0
+    )
     picked = jnp.take(grads_all, jnp.maximum(packed_slot_index, 0), axis=0)
     grad_hidden = jnp.where(active[:, None], picked, zero_row)
     grad_scale = 1.0 / math.sqrt(seq_count * act_rows * lax.axis_size("dp"))

time: 330 us -> 300 us (0.909)
  waiting for transfers between devices: 238 us -> 209 us
    all_gather x1 -> x0, waiting for transfers between devices: 41.4 us -> none  [body(): grads_all = lax.all_gather(gradient_rows, 'seq', axis=0, tiled=True)]
    ppermute x0 -> x3, waiting for transfers between devices: none -> 25 us  [body(): lax.ppermute(ring[-1], 'seq', [(dev, (dev + 1) % 4) for dev in range(4)])]
    reduce_scatter x1, waiting for transfers between devices: 16.2 us -> 3.11 us  [body(): lax.psum_scatter(down_term.astype(jnp.bfloat16), 'seq', scatter_dimension...]
    unnamed x9 -> x8, waiting for transfers between devices: 38 us -> 39.8 us
  transfers between devices with their start and end apart: 8 -> 10, of which waited for: 8 -> 9; matrix products, arithmetic and copies ran while one was open for 8% -> 7% of each run, Pallas kernels for 0% -> 0%
where the time goes in v1:
time: 300 us; the launch traced here: 299 us
  waiting for transfers between devices  209 us (70%)
  blocking collectives  39.9 us (13%)
  matrix products  15.5 us (5%)
  between operations  14.4 us (5%)
  local copies, waits for them, and re-layouts  13.6 us (5%)
  other arithmetic  4.71 us (2%)
    unnamed x8, waiting for transfers between devices  39.8 us
    all_gather x1, waiting for transfers between devices, body(): lax.all_gather(output_weight, 'dp', axis=0, tiled=True)  33.7 us
    reduce_scatter x1, waiting for transfers between devices, body(): lax.psum_scatter(up_mid, 'dp', scatter_dimension=0, tiled=True)  32.4 us
    all_gather x1, waiting for transfers between devices, body(): rows_all = lax.all_gather(hidden, 'seq', axis=0, tiled=True)  30.7 us
    all_gather x1, waiting for transfers between devices, body(): lax.all_gather(value_weight, 'dp', axis=0, tiled=True)  30.5 us
    ppermute x3, waiting for transfers between devices, body(): lax.ppermute(ring[-1], 'seq', [(dev, (dev + 1) % 4) for dev in range(4)])  25 us
    reduce_scatter x1, waiting for transfers between devices, body(): lax.psum_scatter(up_term.astype(jnp.bfloat16), 'seq', scatter_dimension=1...  13.9 us
    all_gather x1, blocking collectives, body(): lax.all_gather(depths, 'seq', axis=0, tiled=True)  12.8 us
  transfers between devices with their start and end apart: 10, of which 9 were waited for; matrix products, arithmetic and copies ran while one was open for 7% of the time, Pallas kernels for 0%

profile of v1, /device:TPU:0, one launch (start us, length us, event | category | flops | bytes accessed | tf_op | source)
XLA Modules:
  0.0 299.2 jit_solution(3460906227836709926)
XLA Ops:
  9.4 12.8 %all-gather = s32[4,1,256]{2,1,0:T(1,128)S(1)} all-gather(s32[1,1,256]{2,1,0:T(1,128)} %bitcast.21), channel_id=1, replica_groups=mesh['dp'=8,'seq'=4] {'seq'}, dimensions={0}, use_global_device_ids=true | all-gather | bytes 5120 | tf_op jit(solution)/shard_map/all_gather | solution.py:93
  22.3 8.1 %all-gather.1 = s32[4,1,256]{2,1,0:T(1,128)S(1)} all-gather(s32[1,1,256]{2,1,0:T(1,128)} %bitcast.20), channel_id=1, replica_groups=mesh['dp'=8,'seq'=4] {'seq'}, dimensions={0}, use_global_device_ids=true | all-gather | bytes 5120 | tf_op jit(solution)/shard_map/all_gather | solution.py:94
  30.4 4.3 %scatter_custom_fusion = s32[128]{0:T(128)S(1)} fusion(s32[1024]{0:T(1024)S(1)} %compare_select_fusion, s32[1024]{0:T(1024)S(1)} %iota.3, s32[]{:T(128)} %constant.88.clone.1), kind=kCustom, calls=%fused_computation.77 | custom fusion | bytes 516 | tf_op jit(solution)/shard_map/scatter | solution.py:106
  34.8 9.5 %all_gather.26 = bf16[1024,128]{1,0:T(8,128)(2,1)S(1)} all-gather(bf16[128,128]{1,0:T(8,128)(2,1)} %param.16), channel_id=1, replica_groups=mesh['dp'=8,'seq'=4] {'dp'}, dimensions={0}, use_global_device_ids=true | all-gather | bytes 294912 | tf_op jit(solution)/shard_map/all_gather | solution.py:90
  44.3 9.5 %all_gather.25 = bf16[1792,128]{1,0:T(8,128)(2,1)S(1)} all-gather(bf16[224,128]{1,0:T(8,128)(2,1)} %param.15), channel_id=1, replica_groups=mesh['dp'=8,'seq'=4] {'dp'}, dimensions={0}, use_global_device_ids=true | all-gather | bytes 516096 | tf_op jit(solution)/shard_map/all_gather | solution.py:89
  53.8 30.7 %all-gather.6.cloned.1.call-done = bf16[1024,1792]{1,0:T(8,128)(2,1)} async-done(((bf16[256,1792]{1,0:T(8,128)(2,1)}), bf16[1024,1792]{1,0:T(8,128)(2,1)}) %all-gather.6.cloned.1.call-update) | async-done | bytes 3670032 | tf_op jit(solution)/shard_map/all_gather | solution.py:102
  84.5 3.8 %gather_fusion = bf16[128,1792]{1,0:T(8,128)(2,1)S(1)} fusion(bf16[1024,1792]{1,0:T(8,128)(2,1)} %all-gather.6.cloned.1.call-done, s32[1024]{0:T(1024)S(1)} %pad_clamp_fusion.1), kind=kCustom, calls=%fused_computation | custom fusion | bytes 918016 | tf_op jit(solution)/shard_map/jit(_take)/gather | solution.py:108
  89.0 30.5 %all-gather.8.cloned.1.call-done = bf16[1792,1024]{1,0:T(8,128)(2,1)} async-done(((bf16[224,1024]{1,0:T(8,128)(2,1)}), bf16[1792,1024]{1,0:T(8,128)(2,1)}) %all-gather.8.cloned.1.call-update) | async-done | bytes 3670032 | tf_op jit(solution)/shard_map/all_gather | solution.py:87
  119.5 2.7 fusion.37
  122.3 33.7 %all-gather.10.cloned.1.call-done = bf16[1024,1792]{1,0:T(8,128)(2,1)} async-done(((bf16[128,1792]{1,0:T(8,128)(2,1)}), bf16[1024,1792]{1,0:T(8,128)(2,1)}) %all-gather.10.cloned.1.call-update) | async-done | bytes 3670032 | tf_op jit(solution)/shard_map/all_gather | solution.py:88
  156.0 2.9 multiply_reduce_fusion
  160.0 3.4 %convolution_convert_fusion = bf16[128,1024]{1,0:T(8,128)(2,1)S(1)} fusion(bf16[1024,1792]{1,0:T(8,128)(2,1)} %all-gather.10.cloned.1.call-done, bf16[128,1792]{1,0:T(8,128)(2,1)S(1)} %copy-done, f32[128,1792]{1,0:T(8,128)S(1)} %get-tuple-element.7, f32[128]{0:T(128)S(1)} %broadcast_multiply_fusion.1, f32[1792]{0:T(1024)S(1)} %copy-done.3, ...), kind=kOutput, calls=%fused_computation.15 | convolution fusion | flops 471498752 | bytes 5316608 | tf_op jit(solution)/shard_map/dot_general | solution.py:11
  164.8 3.4 %fusion.39 = f32[128,1792]{1,0:T(8,128)S(1)} fusion(bf16[128,1024]{1,0:T(8,128)(2,1)S(1)} %convolution_convert_fusion, bf16[1792,1024]{1,0:T(8,128)(2,1)} %all-gather.8.cloned.1.call-done), kind=kOutput, calls=%fused_computation.81 | convolution fusion | flops 469762048 | bytes 4849664 | tf_op jit(solution)/shard_map/dot_general | solution.py:11
  169.4 1.6 collective-permute-start
  172.0 17.7 %collective-permute-done = bf16[128,1792]{1,0:T(8,128)(2,1)S(1)} collective-permute-done((bf16[128,1792]{1,0:T(8,128)(2,1)S(1)}, bf16[128,1792]{1,0:T(8,128)(2,1)S(1)}, u32[]{:S(2)}, u32[]{:S(2)}) %collective-permute-start) | collective-permute-done | bytes 458784 | tf_op jit(solution)/shard_map/ppermute | solution.py:121
  189.7 3.1 %reduce-scatter.7.cloned.1.call-done = bf16[1792,32]{0,1:T(8,128)(2,1)} async-done(((bf16[1792,128]{0,1:T(8,128)(2,1)}), bf16[1792,32]{0,1:T(8,128)(2,1)}) %reduce-scatter.7.cloned.1.call-update) | async-done | bytes 114704 | tf_op jit(solution)/shard_map/reduce_scatter | solution.py:131
  192.8 2.0 copy.14
  194.9 7.3 %collective-permute-done.1 = bf16[128,1792]{1,0:T(8,128)(2,1)S(1)} collective-permute-done((bf16[128,1792]{1,0:T(8,128)(2,1)S(1)}, bf16[128,1792]{1,0:T(8,128)(2,1)S(1)}, u32[]{:S(2)}, u32[]{:S(2)}) %collective-permute-start.1) | collective-permute-done | bytes 458784 | tf_op jit(solution)/shard_map/ppermute | solution.py:121
  202.3 13.9 %reduce-scatter.9.cloned.1.call-done = bf16[1024,32]{0,1:T(8,128)(2,1)} async-done(((bf16[1024,128]{0,1:T(8,128)(2,1)}), bf16[1024,32]{0,1:T(8,128)(2,1)}) %reduce-scatter.9.cloned.1.call-update) | async-done | bytes 65552 | tf_op jit(solution)/shard_map/reduce_scatter | solution.py:134
  216.2 1.5 convert_element_type.55
  217.7 37.7 %reduce-scatter.13.cloned.1.call-done = f32[224,32]{1,0:T(8,128)} async-done(((f32[1792,32]{1,0:T(8,128)}), f32[224,32]{1,0:T(8,128)}) %reduce-scatter.13.cloned.1.call-update) | async-done | bytes 28688
  255.5 1.6 copy.15
  257.5 1.3 gather_fusion.1
  260.0 32.4 %reduce-scatter.11.cloned.1.call-done = f32[128,32]{0,1:T(8,128)} async-done(((f32[1024,32]{0,1:T(8,128)}), f32[128,32]{0,1:T(8,128)}) %reduce-scatter.11.cloned.1.call-update) | async-done | bytes 16400 | tf_op jit(solution)/shard_map/reduce_scatter | solution.py:140
  (64 shorter events, 9.2 us)
Async XLA Ops:
  7.2 81.5 %copy-start.4 = (f32[1792]{0:T(1024)S(1)}, f32[1792]{0:T(1024)}, u32[]{:S(2)}) copy-start(f32[1792]{0:T(1024)} %param.17) | copy-start | bytes 21508
  7.2 77.3 %all-gather.6.cloned.1.call-start = ((), (), s32[]{:S(2)}) async-start(), calls=%async_computation.4 | async-start | bytes 4587520 | tf_op jit(solution)/shard_map/all_gather | solution.py:102
  7.9 111.6 %all-gather.8.cloned.1.call-start = ((), (), s32[]{:S(2)}) async-start(), calls=%async_computation.5 | async-start | bytes 4128768 | tf_op jit(solution)/shard_map/all_gather | solution.py:87
  8.7 147.3 %all-gather.10.cloned.1.call-start = ((), (), s32[]{:S(2)}) async-start(), calls=%async_computation.6 | async-start | bytes 4128768 | tf_op jit(solution)/shard_map/all_gather | solution.py:88
  9.4 183.4 %reduce-scatter.7.cloned.1.call-start = ((), (), s32[]{:S(2)}) async-start(), calls=%async_computation.7 | async-start | bytes 573440 | tf_op jit(solution)/shard_map/reduce_scatter | solution.py:131
  89.0 69.9 %copy-start.1 = (bf16[128,128]{1,0:T(8,128)(2,1)}, bf16[128,128]{1,0:T(8,128)(2,1)S(1)}, u32[]{:S(2)}) copy-start(bf16[128,128]{1,0:T(8,128)(2,1)S(1)} %convolution_convert_fusion.1) | copy-start | bytes 98308
  122.3 36.7 %copy-start = (bf16[128,1792]{1,0:T(8,128)(2,1)S(1)}, bf16[128,1792]{1,0:T(8,128)(2,1)}, u32[]{:S(2)}) copy-start(bf16[128,1792]{1,0:T(8,128)(2,1)} %param.19) | copy-start | bytes 1376260
  122.3 36.7 %copy-start.3 = (f32[1792]{0:T(1024)S(1)}, f32[1792]{0:T(1024)}, u32[]{:S(2)}) copy-start(f32[1792]{0:T(1024)} %param.18) | copy-start | bytes 21508
  168.2 2.8 copy-start.2
  168.2 21.5 %copy-start.5 = (s32[256]{0:T(256)S(1)}, s32[256]{0:T(256)}, u32[]{:S(2)}) copy-start(s32[256]{0:T(256)} %param.12) | copy-start | bytes 3076
  168.2 34.1 %copy-start.6 = (s32[256]{0:T(256)S(1)}, s32[256]{0:T(256)}, u32[]{:S(2)}) copy-start(s32[256]{0:T(256)} %param.11) | copy-start | bytes 3076
  168.7 47.5 %reduce-scatter.9.cloned.1.call-start = ((), (), s32[]{:S(2)}) async-start(), calls=%async_computation.8 | async-start | bytes 327680 | tf_op jit(solution)/shard_map/reduce_scatter | solution.py:134
  169.4 20.3 %collective-permute-start = (bf16[128,1792]{1,0:T(8,128)(2,1)S(1)}, bf16[128,1792]{1,0:T(8,128)(2,1)S(1)}, u32[]{:S(2)}, u32[]{:S(2)}) collective-permute-start(bf16[128,1792]{1,0:T(8,128)(2,1)S(1)} %fusion.13), channel_id=1, source_target_pairs={{0,1},{1,2},{2,3},{3,0},{4,5},{5,6},{6,7},{7,4},{8,9},{9,10},{10,1... | collective-permute-start | bytes 1376264 | tf_op jit(solution)/shard_map/ppermute | solution.py:121
  171.9 83.5 %reduce-scatter.13.cloned.1.call-start = ((), (), s32[]{:S(2)}) async-start(), calls=%async_computation.10 | async-start | bytes 1032192
  189.6 12.6 %collective-permute-start.1 = (bf16[128,1792]{1,0:T(8,128)(2,1)S(1)}, bf16[128,1792]{1,0:T(8,128)(2,1)S(1)}, u32[]{:S(2)}, u32[]{:S(2)}) collective-permute-start(bf16[128,1792]{1,0:T(8,128)(2,1)S(1)} %collective-permute-done), channel_id=1, source_target_pairs={{0,1},{1,2},{2,3},{3,0},{4,5},{5,6},{6,7},{7,4},{8,9},{9,10},{10,1... | collective-permute-start | bytes 1376264 | tf_op jit(solution)/shard_map/ppermute | solution.py:121
  194.8 97.6 %reduce-scatter.11.cloned.1.call-start = ((), (), s32[]{:S(2)}) async-start(), calls=%async_computation.9 | async-start | bytes 147456 | tf_op jit(solution)/shard_map/reduce_scatter | solution.py:140
  202.2 54.8 %collective-permute-start.2 = (bf16[128,1792]{1,0:T(8,128)(2,1)S(1)}, bf16[128,1792]{1,0:T(8,128)(2,1)S(1)}, u32[]{:S(2)}, u32[]{:S(2)}) collective-permute-start(bf16[128,1792]{1,0:T(8,128)(2,1)S(1)} %collective-permute-done.1), channel_id=1, source_target_pairs={{0,1},{1,2},{2,3},{3,0},{4,5},{5,6},{6,7},{7,4},{8,9},{9,10},{10,1... | collective-permute-start | bytes 1376264 | tf_op jit(solution)/shard_map/ppermute | solution.py:121
Sparse Core Ops, SparseCore 0:
  9.6 74.8 all-gather.5
  86.4 33.0 all-gather.7
  121.4 34.5 all-gather.9
  168.8 23.9 reduce-scatter.6
  195.0 21.2 reduce-scatter.8
  219.8 35.5 reduce-scatter.12
  259.0 33.3 reduce-scatter.10
